TPU v7x, 32 devices: a whole 2x2x4 slice. The times are simulated.
32 devices in a mesh: grp: 2 (over y), row: 4 (over x, core), col: 4 (over z).
Axes of the slice: x: 2, y: 2, z: 4, core: 2. Of those that a mesh axis runs over, the one named last changes fastest.
Arguments:
- amplitudes: bfloat16 [32768, 16384], P(('grp', 'row'), 'col'), parts along dimension 0, may hold values from -0.046875 to 0.046875
- cholesky: bfloat16 [1024, 32768], P('row', ('grp', 'col')), parts along dimension 1, may hold values from -1.078125 to 1.078125
- occ_index: int32 [32768], P('grp'), parts along dimension 0, may hold values from 0 to 31
- vir_index: int32 [32768], P('grp'), parts along dimension 0, may hold values from 0 to 511
- eps_occ: float32 [64], P('grp'), parts along dimension 0, may hold values from -2 to -0.3
- eps_vir: float32 [1024], P('grp'), parts along dimension 0, may hold values from 0.2 to 3
Outputs:
- new_amplitudes: bfloat16 [32768, 16384], P(('grp', 'row'), 'col'), parts along dimension 0
There are 2 independent parts, one for each index of `grp`. A program takes and returns all parts, laid end to end along the dimension named above; each array names one. Nothing has to cross between parts.
All inputs are finite; a program needn't handle non-finite values.
Results may differ from a plain program's by a relative error of at most 0.0056.
Values may be sent and summed in bfloat16 or wider, within the bound.
A program may use at most 128 MiB of HBM per device.

v0:
```python
import functools

import jax
import jax.numpy as jnp
from jax import lax
from jax.experimental import pallas as pl
from jax.experimental.pallas import tpu as pltpu
from jax.sharding import PartitionSpec as P

MESH = pl.DeviceIdType.MESH


def pair_gaps(occ_index, vir_index, eps_occ, eps_vir, begin_pair, pair_count):
    occ_rows = lax.dynamic_slice_in_dim(occ_index, begin_pair, pair_count, 0)
    vir_rows = lax.dynamic_slice_in_dim(vir_index, begin_pair, pair_count, 0)
    occ_table = jnp.arange(eps_occ.shape[0], dtype=jnp.int32)
    vir_table = jnp.arange(eps_vir.shape[0], dtype=jnp.int32)
    occ_energy = jnp.sum(
        jnp.where(occ_rows[:, None] == occ_table[None, :], eps_occ[None, :], 0.0), axis=1
    )
    vir_energy = jnp.sum(
        jnp.where(vir_rows[:, None] == vir_table[None, :], eps_vir[None, :], 0.0), axis=1
    )
    return vir_energy - occ_energy


def enter(row_count, col_count, me_row, me_col):
    barrier = pltpu.get_barrier_semaphore()
    for step in range(1, row_count):
        pl.semaphore_signal(
            barrier,
            inc=1,
            device_id={"row": lax.rem(me_row + step, row_count)},
            device_id_type=MESH,
        )
    for condition, where in ((me_col > 0, -1), (me_col < col_count - 1, 1)):

        @pl.when(condition)
        def _():
            pl.semaphore_signal(
                barrier, inc=1, device_id={"col": me_col + where}, device_id_type=MESH
            )

    neighbours = jnp.minimum(me_col, 1) + jnp.minimum(col_count - 1 - me_col, 1)
    pl.semaphore_wait(barrier, row_count - 1 + neighbours)


class Gather:
    def __init__(self, row_count, col_count, pieces, own, rows, held, sems, packed):
        self.packed = packed
        self.row_count, self.col_count, self.pieces = row_count, col_count, pieces
        self.own, self.rows, self.held = own, rows, held
        self.send_line, self.recv_line, self.send_row, self.recv_row, self.keep = sems
        self.me_row, self.me_col = lax.axis_index("row"), lax.axis_index("col")
        self.depth = own.shape[0] // pieces
        self.share = row_count // col_count
        self.width = own.shape[1] // self.share

    def part(self, piece):
        return pl.ds(piece * self.depth, self.depth)

    def block_ref(self, block, piece, mine):
        if mine:
            return self.own.at[self.part(piece), :]
        return self.held.at[block, self.part(piece), :]

    def block_part(self, block, index, piece, mine):
        columns = pl.ds(index * self.width, self.width)
        if mine:
            return self.own.at[self.part(piece), columns]
        return self.held.at[block, self.part(piece), columns]

    def row_ref(self, owner, target, piece):
        if not self.packed:
            return self.rows.at[owner, self.part(piece), :]
        half = self.row_count // 2
        other = lax.rem(owner + target, 2)
        base = target + other * (1 - 2 * lax.rem(target, 2))
        slot = lax.rem(owner - base + self.row_count, self.row_count) // 2 + other * half
        begin = pl.multiple_of(slot * self.depth, self.depth)
        return self.rows.at[piece, pl.ds(begin, self.depth), :]

    def line_copy(self, side, block, hops, piece):
        return pltpu.make_async_remote_copy(
            src_ref=self.block_ref(block, piece, hops == 0),
            dst_ref=self.held.at[block, self.part(piece), :],
            send_sem=self.send_line.at[side, hops, piece],
            recv_sem=self.recv_line.at[side, hops, piece],
            device_id={"col": self.me_col + (1 if side == 0 else -1)},
            device_id_type=MESH,
        )

    def row_copy(self, block, index, piece, mine=False):
        return pltpu.make_async_remote_copy(
            src_ref=self.block_part(block, index, piece, mine),
            dst_ref=self.row_ref(self.me_row, block * self.share + index, piece),
            send_sem=self.send_row.at[block, index, piece],
            recv_sem=self.recv_row.at[self.me_row, piece],
            device_id={"row": block * self.share + index},
            device_id_type=MESH,
        )

    def keep_copy(self, block, index, piece, mine=False):
        return pltpu.make_async_copy(
            self.block_part(block, index, piece, mine),
            self.row_ref(self.me_row, self.me_row, piece),
            self.keep.at[piece],
        )

    def on(self, side):
        return self.me_col < self.col_count - 1 if side == 0 else self.me_col > 0

    def spread(self, block, piece, mine=False):
        for index in range(self.share):
            target = block * self.share + index

            @pl.when(target == self.me_row)
            def _():
                self.keep_copy(block, index, piece, mine).start()

            @pl.when(target != self.me_row)
            def _():
                self.row_copy(block, index, piece, mine).start()

    def begin(self, piece):
        for side in range(2):

            @pl.when(self.on(side))
            def _():
                self.line_copy(side, self.me_col, 0, piece).start()

        self.spread(self.me_col, piece, True)

    def source(self, side, hops):
        block = self.me_col - hops if side == 0 else self.me_col + hops
        exists = self.me_col >= hops if side == 0 else self.me_col + hops < self.col_count
        return block, exists

    def arrive(self, hops, piece):
        for side in range(2):
            block, exists = self.source(side, hops)

            @pl.when(exists)
            def _():
                self.line_copy(side, block, hops - 1, piece).wait_recv()

                if hops < self.col_count - 1:

                    @pl.when(self.on(side))
                    def _():
                        self.line_copy(side, block, hops, piece).start()

                self.spread(block, piece)

    def wait_rows(self, piece):
        for other in range(self.row_count):

            @pl.when(other != self.me_row)
            def _():
                pltpu.make_async_remote_copy(
                    src_ref=self.row_ref(other, self.me_row, piece),
                    dst_ref=self.row_ref(other, self.me_row, piece),
                    send_sem=self.send_row.at[0, 0, piece],
                    recv_sem=self.recv_row.at[other, piece],
                    device_id={"row": other},
                    device_id_type=MESH,
                ).wait_recv()

        for block in range(self.col_count):
            for index in range(self.share):

                @pl.when(block * self.share + index == self.me_row)
                def _():
                    self.keep_copy(block, index, piece).wait()

    def wait_sends(self, piece):
        for side in range(2):
            for hops in range(self.col_count - 1):
                block, exists = self.source(side, hops)

                @pl.when(jnp.logical_and(exists, self.on(side)))
                def _():
                    self.line_copy(side, block, hops, piece).wait_send()

        for block in range(self.col_count):
            for index in range(self.share):

                @pl.when(block * self.share + index != self.me_row)
                def _():
                    self.row_copy(block, index, piece).wait_send()


def gather_sems(row_count, col_count, pieces):
    return [
        pltpu.SemaphoreType.DMA((2, col_count, pieces)),
        pltpu.SemaphoreType.DMA((2, col_count, pieces)),
        pltpu.SemaphoreType.DMA((col_count, row_count // col_count, pieces)),
        pltpu.SemaphoreType.DMA((row_count, pieces)),
        pltpu.SemaphoreType.DMA((pieces,)),
    ]


class Columns:
    def __init__(self, row_count, pieces, own, cols, sems):
        self.row_count, self.pieces, self.own, self.cols = row_count, pieces, own, cols
        self.load, self.send, self.recv, self.send_on = sems
        self.me_row = lax.axis_index("row")
        self.partner = self.me_row + 1 - 2 * lax.rem(self.me_row, 2)
        self.depth = own.shape[0] // pieces

    def part(self, piece):
        return pl.ds(piece * self.depth, self.depth)

    def copy(self, owner, target, sem, piece, src=None):
        dst = self.cols.at[owner, self.part(piece), :]
        return pltpu.make_async_remote_copy(
            src_ref=dst if src is None else src,
            dst_ref=dst,
            send_sem=sem,
            recv_sem=self.recv.at[owner, piece],
            device_id={"row": target},
            device_id_type=MESH,
        )

    def peers(self):
        peers = [(0, self.partner)]
        for step in range(1, self.row_count // 2):
            peers.append((step, lax.rem(self.me_row + 2 * step, self.row_count)))
        return peers

    def first(self, slot, target, piece, src):
        return self.copy(self.me_row, target, self.send.at[slot, piece], piece, src)

    def begin(self, piece, src):
        for slot, target in self.peers():
            self.first(slot, target, piece, src).start()

    def arrive(self, piece):
        for slot, owner in self.peers()[1:]:
            self.copy(owner, self.partner, self.send_on.at[slot, piece], piece).wait_recv()
            self.copy(owner, self.partner, self.send_on.at[slot, piece], piece).start()

    def finish(self, piece, src):
        for slot, target in self.peers():
            self.first(slot, target, piece, src).wait_send()
        self.copy(self.partner, self.partner, self.send.at[0, piece], piece).wait_recv()
        for slot, owner in self.peers()[1:]:
            self.copy(owner, self.partner, self.send_on.at[slot, piece], piece).wait_send()
            theirs = lax.rem(self.partner + 2 * slot, self.row_count)
            self.copy(theirs, self.partner, self.send.at[0, piece], piece).wait_recv()


def columns_sems(row_count, pieces):
    return [
        pltpu.SemaphoreType.DMA((pieces,)),
        pltpu.SemaphoreType.DMA((row_count // 2, pieces)),
        pltpu.SemaphoreType.DMA((row_count, pieces)),
        pltpu.SemaphoreType.DMA((row_count // 2, pieces)),
    ]


def dress_kernel(
    row_count, col_count, pieces, amplitudes, own, held, held_y, y_rows, y_cols, dressed, table, rows, mine, kept,
    to_partner, from_partner, to_peer, from_peer, chol, table_sem, chol_sem,
    partner_send, partner_recv, peer_send, peer_recv, *sems
):
    gather = Gather(row_count, col_count, pieces, own, rows, held, sems[:5], True)
    second = Gather(
        row_count, col_count, pieces, dressed, y_rows, held_y, sems[5:10], False
    )
    columns = Columns(row_count, pieces, dressed, y_cols, sems[10:])
    me_row, depth = gather.me_row, gather.depth
    partner = me_row + 1 - 2 * lax.rem(me_row, 2)
    half = row_count // 2
    split = table_sem.shape[0]
    chunk = table.shape[0] // split
    tile = min(512, table.shape[1])
    tiles = table.shape[1] // tile

    def table_copy(index):
        span = pl.ds(index * chunk, chunk)
        return pltpu.make_async_copy(
            amplitudes.at[span, :], table.at[span, :], table_sem.at[index]
        )

    def chol_copy(piece):
        return pltpu.make_async_copy(
            own.at[gather.part(piece), :], chol.at[piece], chol_sem.at[piece]
        )

    def partner_copy(piece):
        return pltpu.make_async_remote_copy(
            src_ref=to_partner.at[piece % 2],
            dst_ref=from_partner.at[piece],
            send_sem=partner_send.at[piece],
            recv_sem=partner_recv.at[piece],
            device_id={"row": partner},
            device_id_type=MESH,
        )

    def peer_copy(step, piece):
        return pltpu.make_async_remote_copy(
            src_ref=to_peer.at[piece % 2, step - 1],
            dst_ref=from_peer.at[piece, half - step - 1],
            send_sem=peer_send.at[piece, step],
            recv_sem=peer_recv.at[piece, half - step],
            device_id={"row": lax.rem(me_row + 2 * step, row_count)},
            device_id_type=MESH,
        )

    def multiply(piece):
        if piece >= 2:
            partner_copy(piece - 2).wait_send()

        @pl.loop(0, tiles)
        def _(index):
            span = pl.ds(pl.multiple_of(index * tile, tile), tile)
            product = jnp.dot(
                rows[piece], table[:, span], preferred_element_type=jnp.float32
            )
            mine[:, span] = product[: half * depth]
            to_partner[piece % 2, :, span] = product[half * depth :].astype(jnp.bfloat16)

        partner_copy(piece).start()

    def pair(piece):
        partner_copy(piece).wait_recv()
        if piece >= 2:
            for step in range(1, half):
                peer_copy(step, piece - 2).wait_send()

        @pl.loop(0, tiles)
        def _(index):
            span = pl.ds(pl.multiple_of(index * tile, tile), tile)
            both = mine[:, span] + from_partner[piece, :, span].astype(jnp.float32)
            kept[piece % 2, :, span] = both[:depth]
            for step in range(1, half):
                to_peer[piece % 2, step - 1, :, span] = both[
                    step * depth : (step + 1) * depth
                ].astype(jnp.bfloat16)

        for step in range(1, half):
            peer_copy(step, piece).start()

    def close(piece):
        chol_copy(piece).wait()
        for step in range(1, half):
            peer_copy(step, piece).wait_recv()

        @pl.loop(0, tiles)
        def _(index):
            span = pl.ds(pl.multiple_of(index * tile, tile), tile)
            total = kept[piece % 2, :, span]
            for step in range(1, half):
                total = total + from_peer[piece, step - 1, :, span].astype(jnp.float32)
            total = chol[piece, :, span].astype(jnp.float32) + total
            dressed[gather.part(piece), span] = total.astype(jnp.bfloat16)

    def own_y(piece):
        return dressed.at[gather.part(piece), :]

    def own_cols(piece):
        return pltpu.make_async_copy(
            own_y(piece), y_cols.at[me_row, gather.part(piece), :], columns.load.at[piece]
        )

    enter(row_count, col_count, gather.me_row, gather.me_col)
    for piece in range(min(2, pieces)):
        gather.begin(piece)
    for index in range(split):
        table_copy(index).start()
    for piece in range(pieces):
        chol_copy(piece).start()
    for step in range(pieces + 2 * col_count - 1):
        if step + 2 < pieces:
            gather.begin(step + 2)
        for hops in range(1, col_count):
            if 0 <= step - hops + 1 < pieces:
                gather.arrive(hops, step - hops + 1)
        piece = step - (col_count - 2)
        if 0 <= piece - 1 < pieces:
            pair(piece - 1)
        if 0 <= piece - 2 < pieces:
            close(piece - 2)
            second.begin(piece - 2)
            own_cols(piece - 2).start()
            columns.begin(piece - 2, own_y(piece - 2))
        if 0 <= piece < pieces:
            gather.wait_rows(piece)
            if piece == 0:
                for index in range(split):
                    table_copy(index).wait()
            multiply(piece)
        for hops in range(1, col_count):
            if 0 <= step - col_count - hops < pieces:
                second.arrive(hops, step - col_count - hops)
        if 0 <= step - col_count - 1 < pieces:
            columns.arrive(step - col_count - 1)
    for piece in range(pieces):
        gather.wait_sends(piece)
        second.wait_rows(piece)
        second.wait_sends(piece)
        own_cols(piece).wait()
        columns.finish(piece, own_y(piece))
        if piece >= pieces - 2:
            partner_copy(piece).wait_send()
            for step in range(1, half):
                peer_copy(step, piece).wait_send()


def dress_pairs(amplitudes, own, row_count, col_count, collective_id):
    depth, width = own.shape
    pieces = max(1, min(8, depth // 16))
    depth_piece, half = depth // pieces, row_count // 2
    bf16, f32, dma = jnp.bfloat16, jnp.float32, pltpu.SemaphoreType.DMA
    scratch = [
        pltpu.VMEM((depth, width), bf16),
        pltpu.VMEM(amplitudes.shape, bf16),
        pltpu.VMEM((pieces, row_count * depth_piece, amplitudes.shape[0]), bf16),
        pltpu.VMEM((half * depth_piece, width), f32),
        pltpu.VMEM((2, depth_piece, width), f32),
        pltpu.VMEM((2, half * depth_piece, width), bf16),
        pltpu.VMEM((pieces, half * depth_piece, width), bf16),
        pltpu.VMEM((2, half - 1, depth_piece, width), bf16),
        pltpu.VMEM((pieces, half - 1, depth_piece, width), bf16),
        pltpu.VMEM((pieces, depth_piece, width), bf16),
        dma((4,)),
        dma((pieces,)),
        dma((pieces,)),
        dma((pieces,)),
        dma((pieces, half)),
        dma((pieces, half)),
    ]
    scratch += gather_sems(row_count, col_count, pieces) * 2 + columns_sems(row_count, pieces)
    rows_width = amplitudes.shape[0]
    _, _, y_rows, y_cols = pl.pallas_call(
        functools.partial(dress_kernel, row_count, col_count, pieces),
        out_shape=(
            jax.ShapeDtypeStruct((col_count, depth, width), bf16),
            jax.ShapeDtypeStruct((col_count, depth, width), bf16),
            jax.ShapeDtypeStruct((row_count, depth, rows_width), bf16),
            jax.ShapeDtypeStruct((row_count, depth, width), bf16),
        ),
        in_specs=[pl.BlockSpec(memory_space=pl.ANY)] * 2,
        out_specs=(pl.BlockSpec(memory_space=pl.ANY),) * 4,
        scratch_shapes=scratch,
        compiler_params=pltpu.CompilerParams(
            collective_id=collective_id, has_side_effects=True, vmem_limit_bytes=67043328
        ),
        name="dress",
    )(amplitudes, own)
    return (
        y_rows.reshape(row_count * depth, rows_width),
        y_cols.reshape(row_count * depth, width),
    )


def local(row_count, col_count, amplitudes, cholesky, occ_index, vir_index, eps_occ, eps_vir):
    row_position = lax.axis_index("row")
    col_position = lax.axis_index("col")
    rows_block, cols_block = amplitudes.shape
    ydress_rows, ydress_cols = dress_pairs(amplitudes, cholesky, row_count, col_count, 0)
    contract = (((0,), (0,)), ((), ()))
    gram = lax.dot_general(
        ydress_rows, ydress_cols, contract, preferred_element_type=jnp.float32
    )
    gap_rows = pair_gaps(
        occ_index, vir_index, eps_occ, eps_vir, row_position * rows_block, rows_block
    )
    gap_cols = pair_gaps(
        occ_index, vir_index, eps_occ, eps_vir, col_position * cols_block, cols_block
    )
    return (-gram / (gap_rows[:, None] + gap_cols[None, :])).astype(jnp.bfloat16)


def solution(mesh):
    return jax.shard_map(
        functools.partial(local, mesh.shape["row"], mesh.shape["col"]),
        mesh=mesh,
        in_specs=(
            P(("grp", "row"), "col"),
            P("row", ("grp", "col")),
            P("grp"),
            P("grp"),
            P("grp"),
            P("grp"),
        ),
        out_specs=P(("grp", "row"), "col"),
        check_vma=False,
    )
```

profile of v0, /device:TPU:3, one launch (start us, length us, event | category | flops | bytes accessed | tf_op | source)
XLA Modules:
  0.0 368.6 jit_solution(4703888764790450851)
XLA Ops:
  0.0 0.8 fusion.2
  0.8 0.9 select_reduce_fusion.3
  1.7 3.8 %select_reduce_fusion.1 = (f32[4096]{0:T(1024)S(1)}, f32[4096]{0:T(1024)S(1)}) fusion(f32[512]{0:T(512)} %param.11, s32[4096]{0:T(1024)S(1)} %get-tuple-element.17, s32[4096]{0:T(1024)S(1)} %get-tuple-element.18), kind=kLoop, calls=%fused_computation.5 | loop fusion | flops 12574720 | bytes 67584 | tf_op jit(solution)/shard_map/reduce_sum | solution.py:21
  5.5 0.6 sub.14
  6.1 0.6 sub.15
  6.7 313.7 %dress.1 = (bf16[4,256,4096]{2,1,0:T(8,128)(2,1)}, bf16[4,256,4096]{2,1,0:T(8,128)(2,1)}, bf16[4,256,4096]{2,1,0:T(8,128)(2,1)}, bf16[4,256,4096]{2,1,0:T(8,128)(2,1)}) custom-call(bf16[4096,4096]{1,0:T(8,128)(2,1)} %amplitudes.1, bf16[256,4096]{1,0:T(8,128)(2,1)} %own.1), custom_call_target="tpu_custom_call" | custom-call | tf_op jit(solution)/shard_map/dress/pallas_call | solution.py:436
  320.4 48.2 %fusion.1 = bf16[4096,4096]{1,0:T(8,128)(2,1)} fusion(bf16[4,256,4096]{2,1,0:T(8,128)(2,1)} %get-tuple-element.7, bf16[4,256,4096]{2,1,0:T(8,128)(2,1)} %get-tuple-element.8, f32[4096]{0:T(1024)} %sub.15, f32[4096]{0:T(1024)} %sub.14), kind=kOutput, calls=%fused_computation.2 | convolution fusion | flops 34426847232 | bytes 50364416 | tf_op jit(solution)/shard_map/dot_general | solution.py:464
where the time goes:
time: 369 us
  Pallas kernels  314 us (85%)
  matrix products  48.2 us (13%)
  other arithmetic  5.91 us (2%)
    pallas_call x1, Pallas kernels, dress_pairs(): pl.pallas_call(functools.partial(dress_kernel, row_count, col_count, piec...  314 us
    dot_general x1, matrix products, local(): lax.dot_general(ydress_rows, ydress_cols, contract, preferred_element_typ...  48.2 us

commit v1 on v0

--- a/solution.py
+++ b/solution.py
@@ -46,8 +46,7 @@
 
 
 class Gather:
-    def __init__(self, row_count, col_count, pieces, own, rows, held, sems, packed):
-        self.packed = packed
+    def __init__(self, row_count, col_count, pieces, own, rows, held, sems):
         self.row_count, self.col_count, self.pieces = row_count, col_count, pieces
         self.own, self.rows, self.held = own, rows, held
         self.send_line, self.recv_line, self.send_row, self.recv_row, self.keep = sems
@@ -71,8 +70,6 @@
         return self.held.at[block, self.part(piece), columns]
 
     def row_ref(self, owner, target, piece):
-        if not self.packed:
-            return self.rows.at[owner, self.part(piece), :]
         half = self.row_count // 2
         other = lax.rem(owner + target, 2)
         base = target + other * (1 - 2 * lax.rem(target, 2))
@@ -259,15 +256,168 @@
     ]
 
 
+class Chunks:
+    def __init__(self, row_count, col_count, chunks, own, rows, held, sems):
+        self.row_count, self.col_count, self.chunks = row_count, col_count, chunks
+        self.own, self.rows, self.held = own, rows, held
+        self.send_line, self.recv_line, self.send_row, self.recv_row, self.keep = sems
+        self.me_row, self.me_col = lax.axis_index("row"), lax.axis_index("col")
+        self.share = row_count // col_count
+        self.pieces = chunks * self.share
+        self.depth = own.shape[0]
+        self.width = own.shape[1] // self.pieces
+
+    def block_ref(self, block, chunk, index, mine):
+        if mine:
+            begin = pl.multiple_of((index * self.chunks + chunk) * self.width, self.width)
+            return self.own.at[:, pl.ds(begin, self.width)]
+        return self.held.at[block, chunk * self.share + index]
+
+    def row_ref(self, owner, chunk):
+        begin = pl.multiple_of(owner * self.depth, self.depth)
+        return self.rows.at[chunk, pl.ds(begin, self.depth), :]
+
+    def line_copy(self, side, block, hops, chunk, index, mine=False):
+        piece = chunk * self.share + index
+        return pltpu.make_async_remote_copy(
+            src_ref=self.block_ref(block, chunk, index, mine),
+            dst_ref=self.held.at[block, piece],
+            send_sem=self.send_line.at[side, hops, piece],
+            recv_sem=self.recv_line.at[side, hops, piece],
+            device_id={"col": self.me_col + (1 if side == 0 else -1)},
+            device_id_type=MESH,
+        )
+
+    def row_copy(self, block, chunk, index, mine=False):
+        return pltpu.make_async_remote_copy(
+            src_ref=self.block_ref(block, chunk, index, mine),
+            dst_ref=self.row_ref(self.me_row, chunk),
+            send_sem=self.send_row.at[block, chunk * self.share + index],
+            recv_sem=self.recv_row.at[self.me_row, chunk],
+            device_id={"row": block * self.share + index},
+            device_id_type=MESH,
+        )
+
+    def keep_copy(self, block, chunk, index, mine=False):
+        return pltpu.make_async_copy(
+            self.block_ref(block, chunk, index, mine),
+            self.row_ref(self.me_row, chunk),
+            self.keep.at[chunk],
+        )
+
+    def on(self, side):
+        return self.me_col < self.col_count - 1 if side == 0 else self.me_col > 0
+
+    def spread(self, block, chunk, index, mine=False):
+        target = block * self.share + index
+
+        @pl.when(target == self.me_row)
+        def _():
+            self.keep_copy(block, chunk, index, mine).start()
+
+        @pl.when(target != self.me_row)
+        def _():
+            self.row_copy(block, chunk, index, mine).start()
+
+    def begin(self, chunk):
+        for index in range(self.share):
+            for side in range(2):
+
+                @pl.when(self.on(side))
+                def _():
+                    self.line_copy(side, self.me_col, 0, chunk, index, True).start()
+
+            self.spread(self.me_col, chunk, index, True)
+
+    def source(self, side, hops):
+        block = self.me_col - hops if side == 0 else self.me_col + hops
+        exists = self.me_col >= hops if side == 0 else self.me_col + hops < self.col_count
+        return block, exists
+
+    def arrive(self, hops, chunk):
+        for side in range(2):
+            block, exists = self.source(side, hops)
+
+            @pl.when(exists)
+            def _():
+                for index in range(self.share):
+                    self.line_copy(side, block, hops - 1, chunk, index).wait_recv()
+
+                    @pl.when(jnp.logical_and(self.on(side), hops < self.col_count - 1))
+                    def _():
+                        self.line_copy(side, block, hops, chunk, index).start()
+
+                    self.spread(block, chunk, index)
+
+    def wait_rows(self, chunk):
+        for other in range(self.row_count):
+
+            @pl.when(other != self.me_row)
+            def _():
+                pltpu.make_async_remote_copy(
+                    src_ref=self.row_ref(other, chunk),
+                    dst_ref=self.row_ref(other, chunk),
+                    send_sem=self.send_row.at[0, 0],
+                    recv_sem=self.recv_row.at[other, chunk],
+                    device_id={"row": other},
+                    device_id_type=MESH,
+                ).wait_recv()
+
+        pltpu.make_async_copy(
+            self.row_ref(self.me_row, chunk), self.row_ref(self.me_row, chunk), self.keep.at[chunk]
+        ).wait()
+
+    def wait_sends(self, chunk):
+        for index in range(self.share):
+            for side in range(2):
+                for hops in range(self.col_count - 1):
+                    block, exists = self.source(side, hops)
+
+                    @pl.when(jnp.logical_and(exists, self.on(side)))
+                    def _():
+                        self.line_copy(side, self.me_col, hops, chunk, index).wait_send()
+
+            for block in range(self.col_count):
+
+                @pl.when(block * self.share + index != self.me_row)
+                def _():
+                    self.row_copy(block, chunk, index).wait_send()
+
+
+def chunk_sems(row_count, col_count, chunks):
+    pieces = chunks * (row_count // col_count)
+    return [
+        pltpu.SemaphoreType.DMA((2, col_count, pieces)),
+        pltpu.SemaphoreType.DMA((2, col_count, pieces)),
+        pltpu.SemaphoreType.DMA((col_count, pieces)),
+        pltpu.SemaphoreType.DMA((row_count, chunks)),
+        pltpu.SemaphoreType.DMA((chunks,)),
+    ]
+
+
+def turn(chunk_ref, turned, gap_rows, gap_turned, begin):
+    rows = turned.shape[0]
+    turned[...] = chunk_ref[...].T
+    gaps = gap_rows[:, pl.ds(pl.multiple_of(begin, rows), rows)]
+    gap_turned[...] = jnp.broadcast_to(gaps, (128, rows)).T
+
+
+def quotient(turned, right, gap_turned, gap_cols, span):
+    gram = jnp.dot(turned[...], right, preferred_element_type=jnp.float32)
+    copies = gram.shape[1] // 128
+    total = jnp.concatenate([gap_turned[...]] * copies, axis=1) + gap_cols[:, span]
+    return (-gram / total).astype(jnp.bfloat16)
+
+
 def dress_kernel(
-    row_count, col_count, pieces, amplitudes, own, held, held_y, y_rows, y_cols, dressed, table, rows, mine, kept,
-    to_partner, from_partner, to_peer, from_peer, chol, table_sem, chol_sem,
-    partner_send, partner_recv, peer_send, peer_recv, *sems
+    row_count, col_count, pieces, chunks, ready, amplitudes, own, gap_rows, gap_cols,
+    held, held_y, y_rows, y_cols, done, dressed, table, rows, mine, kept,
+    to_partner, from_partner, to_peer, from_peer, chol, chunk_buf, turned, gap_turned, staged,
+    table_sem, chol_sem, partner_send, partner_recv, peer_send, peer_recv,
+    right_sem, chunk_sem, staged_sem, *sems
 ):
-    gather = Gather(row_count, col_count, pieces, own, rows, held, sems[:5], True)
-    second = Gather(
-        row_count, col_count, pieces, dressed, y_rows, held_y, sems[5:10], False
-    )
+    gather = Gather(row_count, col_count, pieces, own, rows, held, sems[:5])
+    second = Chunks(row_count, col_count, chunks, dressed, y_rows, held_y, sems[5:10])
     columns = Columns(row_count, pieces, dressed, y_cols, sems[10:])
     me_row, depth = gather.me_row, gather.depth
     partner = me_row + 1 - 2 * lax.rem(me_row, 2)
@@ -364,6 +514,39 @@
             own_y(piece), y_cols.at[me_row, gather.part(piece), :], columns.load.at[piece]
         )
 
+    full = dressed.shape[0]
+
+    def right_copy(owner):
+        return pltpu.make_async_copy(
+            y_cols.at[owner], table.at[pl.ds(owner * full, full), :], right_sem.at[owner]
+        )
+
+    def chunk_copy(index):
+        return pltpu.make_async_copy(y_rows.at[index], chunk_buf, chunk_sem.at[0])
+
+    def staged_copy(index, at):
+        slot = lax.rem(at, 2)
+        begin = pl.multiple_of(index * second.width, second.width)
+        span = pl.ds(pl.multiple_of(at * tile, tile), tile)
+        return pltpu.make_async_copy(
+            staged.at[slot], done.at[pl.ds(begin, second.width), span], staged_sem.at[slot]
+        )
+
+    def divide(index):
+        chunk_copy(index).wait()
+        turn(chunk_buf, turned, gap_rows, gap_turned, index * second.width)
+
+        @pl.loop(0, tiles)
+        def _(at):
+            @pl.when(jnp.logical_or(index > 0, at >= 2))
+            def _():
+                staged_copy(index, at).wait()
+
+            span = pl.ds(pl.multiple_of(at * tile, tile), tile)
+            right = table[: row_count * full, span]
+            staged[lax.rem(at, 2)] = quotient(turned, right, gap_turned, gap_cols, span)
+            staged_copy(index, at).start()
+
     enter(row_count, col_count, gather.me_row, gather.me_col)
     for piece in range(min(2, pieces)):
         gather.begin(piece)
@@ -371,7 +554,7 @@
         table_copy(index).start()
     for piece in range(pieces):
         chol_copy(piece).start()
-    for step in range(pieces + 2 * col_count - 1):
+    for step in range(pieces + col_count):
         if step + 2 < pieces:
             gather.begin(step + 2)
         for hops in range(1, col_count):
@@ -382,7 +565,6 @@
             pair(piece - 1)
         if 0 <= piece - 2 < pieces:
             close(piece - 2)
-            second.begin(piece - 2)
             own_cols(piece - 2).start()
             columns.begin(piece - 2, own_y(piece - 2))
         if 0 <= piece < pieces:
@@ -391,26 +573,147 @@
                 for index in range(split):
                     table_copy(index).wait()
             multiply(piece)
-        for hops in range(1, col_count):
-            if 0 <= step - col_count - hops < pieces:
-                second.arrive(hops, step - col_count - hops)
         if 0 <= step - col_count - 1 < pieces:
             columns.arrive(step - col_count - 1)
+
+    @pl.loop(0, chunks)
+    def _(index):
+        second.begin(index)
+
+    columns.arrive(pieces - 1)
+    for piece in range(pieces):
+        own_cols(piece).wait()
+        columns.finish(piece, own_y(piece))
+    for owner in range(row_count):
+        right_copy(owner).start()
+
+    turn_at = jnp.maximum(jnp.abs(gather.me_col - me_row // second.share), 1)
+
+    @pl.loop(0, (col_count - 1) * chunks)
+    def _(step):
+        hops = lax.div(step, chunks) + 1
+        index = lax.rem(step, chunks)
+        go = jnp.logical_and(hops == turn_at, jnp.logical_and(index > 0, index <= ready))
+
+        @pl.when(go)
+        def _():
+            second.wait_rows(index - 1)
+            chunk_copy(index - 1).start()
+
+        second.arrive(hops, index)
+
+        @pl.when(go)
+        def _():
+            @pl.when(index == 1)
+            def _():
+                for owner in range(row_count):
+                    right_copy(owner).wait()
+
+            divide(index - 1)
+
+    for at in range(2):
+        staged_copy(0, at).wait()
     for piece in range(pieces):
         gather.wait_sends(piece)
-        second.wait_rows(piece)
-        second.wait_sends(piece)
-        own_cols(piece).wait()
-        columns.finish(piece, own_y(piece))
         if piece >= pieces - 2:
             partner_copy(piece).wait_send()
             for step in range(1, half):
                 peer_copy(step, piece).wait_send()
 
-
-def dress_pairs(amplitudes, own, row_count, col_count, collective_id):
+    for index in range(ready, chunks):
+        second.wait_rows(index)
+
+    @pl.loop(0, chunks)
+    def _(index):
+        second.wait_sends(index)
+
+
+def finish_kernel(
+    row_count, ready, done, y_rows, y_cols, gap_rows, gap_cols, out,
+    passed, right, chunk_buf, turned, gap_turned, staged,
+    right_sem, chunk_sem, read_sem, write_sem, staged_sem
+):
+    full = y_cols.shape[1]
+    late = chunk_buf.shape[0]
+    rows, tile = staged.shape[1:]
+    tiles = right.shape[1] // tile
+    part = passed.shape[1]
+
+    def right_copy(owner):
+        return pltpu.make_async_copy(
+            y_cols.at[owner], right.at[pl.ds(owner * full, full), :], right_sem.at[owner]
+        )
+
+    def chunk_copy(index):
+        return pltpu.make_async_copy(
+            y_rows.at[ready + index], chunk_buf.at[index], chunk_sem.at[index]
+        )
+
+    def read(index):
+        begin = pl.multiple_of(index * part, part)
+        return pltpu.make_async_copy(
+            done.at[pl.ds(begin, part), :], passed.at[index], read_sem.at[index]
+        )
+
+    def write(index):
+        begin = pl.multiple_of(index * part, part)
+        return pltpu.make_async_copy(
+            passed.at[index], out.at[pl.ds(begin, part), :], write_sem.at[index]
+        )
+
+    def staged_copy(index, at):
+        slot = lax.rem(at, 2)
+        span = pl.ds(pl.multiple_of(at * tile, tile), tile)
+        return pltpu.make_async_copy(
+            staged.at[slot], out.at[pl.ds((ready + index) * rows, rows), span], staged_sem.at[slot]
+        )
+
+    for owner in range(row_count):
+        right_copy(owner).start()
+    for index in range(late):
+        chunk_copy(index).start()
+
+    @pl.loop(0, late * tiles)
+    def _(index):
+        read(index).start()
+
+    for owner in range(row_count):
+        right_copy(owner).wait()
+    for index in range(late):
+        chunk_copy(index).wait()
+        turn(chunk_buf.at[index], turned, gap_rows, gap_turned, (ready + index) * rows)
+
+        @pl.loop(0, tiles)
+        def _(at):
+            read(index * tiles + at).wait()
+            write(index * tiles + at).start()
+
+            @pl.when(jnp.logical_or(index > 0, at >= 2))
+            def _():
+                staged_copy(index, at).wait()
+
+            span = pl.ds(pl.multiple_of(at * tile, tile), tile)
+            staged[lax.rem(at, 2)] = quotient(turned, right[:, span], gap_turned, gap_cols, span)
+            staged_copy(index, at).start()
+
+    for at in range(2):
+        staged_copy(0, at).wait()
+
+    @pl.loop(0, late * tiles)
+    def _(index):
+        write(index).wait()
+
+
+def update(amplitudes, own, gap_rows, gap_cols, row_count, col_count, collective_id):
     depth, width = own.shape
+    rows_width = amplitudes.shape[0]
     pieces = max(1, min(8, depth // 16))
+    chunks = max(2, min(8, rows_width // 128))
+    late = max(1, chunks // 4)
+    ready = chunks - late
+    share = row_count // col_count
+    span = rows_width // chunks
+    tile = min(512, width)
     depth_piece, half = depth // pieces, row_count // 2
     bf16, f32, dma = jnp.bfloat16, jnp.float32, pltpu.SemaphoreType.DMA
     scratch = [
@@ -424,53 +727,78 @@
         pltpu.VMEM((2, half - 1, depth_piece, width), bf16),
         pltpu.VMEM((pieces, half - 1, depth_piece, width), bf16),
         pltpu.VMEM((pieces, depth_piece, width), bf16),
+        pltpu.VMEM((row_count * depth, span), bf16),
+        pltpu.VMEM((span, row_count * depth), bf16),
+        pltpu.VMEM((span, 128), f32),
+        pltpu.VMEM((2, span, tile), bf16),
         dma((4,)),
         dma((pieces,)),
         dma((pieces,)),
         dma((pieces,)),
         dma((pieces, half)),
         dma((pieces, half)),
+        dma((row_count,)),
+        dma((1,)),
+        dma((2,)),
     ]
-    scratch += gather_sems(row_count, col_count, pieces) * 2 + columns_sems(row_count, pieces)
-    rows_width = amplitudes.shape[0]
-    _, _, y_rows, y_cols = pl.pallas_call(
-        functools.partial(dress_kernel, row_count, col_count, pieces),
+    scratch += gather_sems(row_count, col_count, pieces)
+    scratch += chunk_sems(row_count, col_count, chunks) + columns_sems(row_count, pieces)
+    anywhere = pl.BlockSpec(memory_space=pl.ANY)
+    near = pl.BlockSpec(memory_space=pltpu.VMEM)
+    _, _, y_rows, y_cols, done = pl.pallas_call(
+        functools.partial(dress_kernel, row_count, col_count, pieces, chunks, ready),
         out_shape=(
             jax.ShapeDtypeStruct((col_count, depth, width), bf16),
-            jax.ShapeDtypeStruct((col_count, depth, width), bf16),
-            jax.ShapeDtypeStruct((row_count, depth, rows_width), bf16),
+            jax.ShapeDtypeStruct((col_count, chunks * share, depth, span), bf16),
+            jax.ShapeDtypeStruct((chunks, row_count * depth, span), bf16),
             jax.ShapeDtypeStruct((row_count, depth, width), bf16),
+            jax.ShapeDtypeStruct((ready * span, width), bf16),
         ),
-        in_specs=[pl.BlockSpec(memory_space=pl.ANY)] * 2,
-        out_specs=(pl.BlockSpec(memory_space=pl.ANY),) * 4,
+        in_specs=[anywhere, anywhere, near, near],
+        out_specs=(anywhere,) * 5,
         scratch_shapes=scratch,
         compiler_params=pltpu.CompilerParams(
             collective_id=collective_id, has_side_effects=True, vmem_limit_bytes=67043328
         ),
         name="dress",
-    )(amplitudes, own)
-    return (
-        y_rows.reshape(row_count * depth, rows_width),
-        y_cols.reshape(row_count * depth, width),
-    )
+    )(amplitudes, own, gap_rows, gap_cols)
+    moves = late * (width // tile)
+    return pl.pallas_call(
+        functools.partial(finish_kernel, row_count, ready),
+        out_shape=jax.ShapeDtypeStruct(amplitudes.shape, bf16),
+        in_specs=[anywhere] * 3 + [near] * 2,
+        out_specs=anywhere,
+        scratch_shapes=[
+            pltpu.VMEM((moves, ready * span // moves, width), bf16),
+            pltpu.VMEM((row_count * depth, width), bf16),
+            pltpu.VMEM((late, row_count * depth, span), bf16),
+            pltpu.VMEM((span, row_count * depth), bf16),
+            pltpu.VMEM((span, 128), f32),
+            pltpu.VMEM((2, span, tile), bf16),
+            dma((row_count,)),
+            dma((late,)),
+            dma((moves,)),
+            dma((moves,)),
+            dma((2,)),
+        ],
+        compiler_params=pltpu.CompilerParams(vmem_limit_bytes=67043328),
+        name="finish",
+    )(done, y_rows, y_cols, gap_rows, gap_cols)
 
 
 def local(row_count, col_count, amplitudes, cholesky, occ_index, vir_index, eps_occ, eps_vir):
     row_position = lax.axis_index("row")
     col_position = lax.axis_index("col")
     rows_block, cols_block = amplitudes.shape
-    ydress_rows, ydress_cols = dress_pairs(amplitudes, cholesky, row_count, col_count, 0)
-    contract = (((0,), (0,)), ((), ()))
-    gram = lax.dot_general(
-        ydress_rows, ydress_cols, contract, preferred_element_type=jnp.float32
-    )
     gap_rows = pair_gaps(
         occ_index, vir_index, eps_occ, eps_vir, row_position * rows_block, rows_block
     )
     gap_cols = pair_gaps(
         occ_index, vir_index, eps_occ, eps_vir, col_position * cols_block, cols_block
     )
-    return (-gram / (gap_rows[:, None] + gap_cols[None, :])).astype(jnp.bfloat16)
+    return update(
+        amplitudes, cholesky, gap_rows[None, :], gap_cols[None, :], row_count, col_count, 0
+    )
 
 
 def solution(mesh):

time: 369 us -> 486 us (1.32)
  Pallas kernels: 314 us -> 478 us
  matrix products: 48.2 us -> 0 us
    pallas_call x1 -> x2, Pallas kernels: 314 us -> 478 us  [the longest x1 454 us: update(): pl.pallas_call(functools.partial(dress_kernel, row_count, col_count, piec...]
    dot_general x1 -> x0, matrix products: 48.2 us -> none  [local(): lax.dot_general(ydress_rows, ydress_cols, contract, preferred_element_typ...]
where the time goes in v1:
time: 486 us; the launch traced here: 485 us
  Pallas kernels  478 us (98%)
  other arithmetic  5.91 us (1%)
    pallas_call x1, Pallas kernels, update(): pl.pallas_call(functools.partial(dress_kernel, row_count, col_count, piec...  454 us
    pallas_call x1, Pallas kernels, update(): pl.pallas_call(functools.partial(finish_kernel, row_count, ready), out_sh...  23.7 us

profile of v1, /device:TPU:3, one launch (start us, length us, event | category | flops | bytes accessed | tf_op | source)
XLA Modules:
  0.0 484.8 jit_solution(3308659882886743626)
XLA Ops:
  0.0 0.8 fusion
  0.8 0.9 select_reduce_fusion.2
  1.7 3.8 select_reduce_fusion
  5.5 0.6 sub.28
  6.1 0.6 sub.26
  6.7 454.2 %dress.1 = (bf16[4,256,4096]{2,1,0:T(8,128)(2,1)}, bf16[4,8,256,512]{3,2,1,0:T(8,128)(2,1)}, bf16[8,1024,512]{2,1,0:T(8,128)(2,1)}, bf16[4,256,4096]{2,1,0:T(8,128)(2,1)}, bf16[3072,4096]{1,0:T(8,128)(2,1)}) custom-call(bf16[4096,4096]{1,0:T(8,128)(2,1)} %amplitudes.1, bf16[256,4096]{1,0:T(8,128)(2,1)} %own.1, f32[1,4096]{1,0:T(1,128)} %bitcast.4, ...), custom_call_target="tpu_custom_call" | custom-call | tf_op jit(solution)/shard_map/dress/pallas_call | solution.py:748
  460.9 23.7 %finish.1 = bf16[4096,4096]{1,0:T(8,128)(2,1)} custom-call(bf16[3072,4096]{1,0:T(8,128)(2,1)} %get-tuple-element.8.done, bf16[8,1024,512]{2,1,0:T(8,128)(2,1)} %get-tuple-element.9.y_rows, bf16[4,256,4096]{2,1,0:T(8,128)(2,1)} %get-tuple-element.10.y_cols, f32[1,4096]{1,0:T(1,128)} %bitcast.5, f32[1,4096]{1,0:T(1,128)} %bitcast.3), custom_call_target="tpu_custom_call" | custom-call | tf_op jit(solution)/shard_map/finish/pallas_call | solution.py:766

commit v2 on v0

v2 whole, which is shorter than its diff:
```python
import functools

import jax
import jax.numpy as jnp
from jax import lax
from jax.experimental import pallas as pl
from jax.experimental.pallas import tpu as pltpu
from jax.sharding import PartitionSpec as P

MESH = pl.DeviceIdType.MESH
CUTS = 1
CHUNKS = 8
LATE = 2
SPLIT = 2
PLAIN = 4
PLAIN_CHUNKS = 4
LAUNCH_LEAD = 1
BEGIN_LEAD = 2
CLOSE_LAG = 1


def pair_gaps(occ_index, vir_index, eps_occ, eps_vir, begin_pair, pair_count):
    occ_rows = lax.dynamic_slice_in_dim(occ_index, begin_pair, pair_count, 0)
    vir_rows = lax.dynamic_slice_in_dim(vir_index, begin_pair, pair_count, 0)
    occ_table = jnp.arange(eps_occ.shape[0], dtype=jnp.int32)
    vir_table = jnp.arange(eps_vir.shape[0], dtype=jnp.int32)
    occ_energy = jnp.sum(
        jnp.where(occ_rows[:, None] == occ_table[None, :], eps_occ[None, :], 0.0), axis=1
    )
    vir_energy = jnp.sum(
        jnp.where(vir_rows[:, None] == vir_table[None, :], eps_vir[None, :], 0.0), axis=1
    )
    return vir_energy - occ_energy


def enter(row_count, col_count, me_row, me_col):
    barrier = pltpu.get_barrier_semaphore()
    for step in range(1, row_count):
        pl.semaphore_signal(
            barrier,
            inc=1,
            device_id={"row": lax.rem(me_row + step, row_count)},
            device_id_type=MESH,
        )
    for condition, where in ((me_col > 0, -1), (me_col < col_count - 1, 1)):

        @pl.when(condition)
        def _():
            pl.semaphore_signal(
                barrier, inc=1, device_id={"col": me_col + where}, device_id_type=MESH
            )

    neighbours = jnp.minimum(me_col, 1) + jnp.minimum(col_count - 1 - me_col, 1)
    pl.semaphore_wait(barrier, row_count - 1 + neighbours)


class Spread:
    def __init__(self, row_count, col_count, own, rows, held, sems):
        self.row_count, self.col_count = row_count, col_count
        self.own, self.rows, self.held = own, rows, held
        self.send_line, self.recv_line, self.send_row, self.recv_row, self.keep = sems[:5]
        self.send_chain, self.recv_chain = sems[5:]
        self.me_row, self.me_col = lax.axis_index("row"), lax.axis_index("col")
        self.share = row_count // col_count
        home = lax.div(self.me_row, self.share)
        ahead = 1 - 2 * lax.rem(home, 2)
        self.after = self.me_col + ahead
        self.onward = jnp.logical_and(self.after >= 0, self.after < col_count)
        self.distance = (self.me_col - home) * ahead
        self.parts = self.send_chain.shape[1]

    def on(self, side):
        return self.me_col < self.col_count - 1 if side == 0 else self.me_col > 0

    def carried(self, block, side, piece):
        return jnp.logical_or(lax.rem(block + side, 2) == 1, self.plain(piece))

    def source(self, side, hops, piece):
        block = self.me_col - hops if side == 0 else self.me_col + hops
        exists = self.me_col >= hops if side == 0 else self.me_col + hops < self.col_count
        return block, jnp.logical_and(exists, self.carried(block + 2 * hops, side, piece))

    def spread_here(self, block, piece):
        side = jnp.where(block < self.me_col, 0, 1)
        return jnp.logical_or(block == self.me_col, self.carried(block, side, piece))

    def spread(self, block, piece, index, mine=False):
        target = block * self.share + index

        @pl.when(target == self.me_row)
        def _():
            self.keep_copy(block, piece, index, mine).start()

        @pl.when(target != self.me_row)
        def _():
            self.row_copy(block, piece, index, mine).start()

    def begin(self, piece):
        for side in range(2):

            @pl.when(jnp.logical_and(self.on(side), self.carried(self.me_col, side, piece)))
            def _():
                for copy in self.line_copies(side, self.me_col, 0, piece, True):
                    copy.start()

        for index in range(self.share):
            self.spread(self.me_col, piece, index, True)

    def arrive(self, hops, piece):
        for side in range(2):
            block, exists = self.source(side, hops, piece)

            @pl.when(exists)
            def _():
                for copy in self.line_copies(side, block, hops - 1, piece):
                    copy.wait_recv()

                if hops < self.col_count - 1:

                    @pl.when(self.on(side))
                    def _():
                        for copy in self.line_copies(side, block, hops, piece):
                            copy.start()

                for index in range(self.share):
                    self.spread(block, piece, index)

    def line_copies(self, side, block, hops, piece, mine=False):
        return [
            pltpu.make_async_remote_copy(
                src_ref=self.block_ref(block, piece, index, mine),
                dst_ref=self.block_ref(block, piece, index, False),
                send_sem=self.send_line.at[side, hops, piece, index],
                recv_sem=self.recv_line.at[side, hops, piece, index],
                device_id={"col": self.me_col + (1 if side == 0 else -1)},
                device_id_type=MESH,
            )
            for index in range(self.share)
        ]

    def row_copy(self, block, piece, index, mine=False):
        target = block * self.share + index
        return pltpu.make_async_remote_copy(
            src_ref=self.block_ref(block, piece, index, mine),
            dst_ref=self.row_ref(self.me_row, target, piece),
            send_sem=self.send_row.at[block, index, piece],
            recv_sem=self.recv_row.at[self.me_row, piece],
            device_id={"row": target},
            device_id_type=MESH,
        )

    def keep_copy(self, block, piece, index, mine=False):
        return pltpu.make_async_copy(
            self.block_ref(block, piece, index, mine),
            self.row_ref(self.me_row, self.me_row, piece),
            self.keep.at[piece],
        )

    def chain_copy(self, piece, part):
        ref = self.chain_ref(piece, part)
        return pltpu.make_async_remote_copy(
            src_ref=ref,
            dst_ref=ref,
            send_sem=self.send_chain.at[piece, part],
            recv_sem=self.recv_chain.at[piece, part],
            device_id={"col": self.after},
            device_id_type=MESH,
        )

    def wait_rows(self, piece):
        mine = self.row_ref(self.me_row, self.me_row, piece)
        for other in range(self.row_count):

            @pl.when(other != self.me_row)
            def _():
                theirs = self.row_ref(other, self.me_row, piece)
                pltpu.make_async_remote_copy(
                    src_ref=theirs,
                    dst_ref=theirs,
                    send_sem=self.send_row.at[0, 0, piece],
                    recv_sem=self.recv_row.at[other, piece],
                    device_id={"row": other},
                    device_id_type=MESH,
                ).wait_recv()

        pltpu.make_async_copy(mine, mine, self.keep.at[piece]).wait()

    def launch(self, piece):
        @pl.when(self.distance == 0)
        def _():
            self.wait_rows(piece)

            @pl.when(jnp.logical_and(self.onward, jnp.logical_not(self.plain(piece))))
            def _():
                for part in range(self.parts):
                    self.chain_copy(piece, part).start()

    def relay(self, distance, piece):
        @pl.when(jnp.logical_and(self.distance == distance, jnp.logical_not(self.plain(piece))))
        def _():
            for part in range(self.parts):
                self.chain_copy(piece, part).wait_recv()

                @pl.when(self.onward)
                def _():
                    self.chain_copy(piece, part).start()

    def sliced(self, piece):
        plain = jnp.logical_and(self.distance > 0, self.plain(piece))
        return jnp.logical_or(self.distance < 0, plain)

    def settle(self, piece):
        self.relay(self.col_count - 1, piece)

        @pl.when(self.sliced(piece))
        def _():
            self.wait_rows(piece)

    def wait_sends(self, piece):
        for side in range(2):
            for hops in range(self.col_count - 1):
                block, exists = self.source(side, hops, piece)

                @pl.when(jnp.logical_and(exists, self.on(side)))
                def _():
                    for copy in self.line_copies(side, self.me_col, hops, piece):
                        copy.wait_send()

        for block in range(self.col_count):
            for index in range(self.share):

                @pl.when(
                    jnp.logical_and(
                        self.spread_here(block, piece), block * self.share + index != self.me_row
                    )
                )
                def _():
                    self.row_copy(block, piece, index).wait_send()

        chained = jnp.logical_and(self.distance >= 0, jnp.logical_not(self.plain(piece)))

        @pl.when(jnp.logical_and(chained, self.onward))
        def _():
            for part in range(self.parts):
                self.chain_copy(piece, part).wait_send()


class Gather(Spread):
    def __init__(self, row_count, col_count, pieces, cuts, own, rows, held, sems):
        super().__init__(row_count, col_count, own, rows, held, sems)
        self.pieces, self.cuts = pieces, cuts
        self.depth = own.shape[0] // pieces
        self.full = own.shape[1] // self.share
        self.width = self.full // cuts

    def plain(self, unit):
        return unit < self.pieces * self.cuts * PLAIN // 8

    def part(self, piece):
        return pl.ds(pl.multiple_of(piece * self.depth, self.depth), self.depth)

    def span(self, unit, index=0):
        begin = index * self.full + lax.rem(unit, self.cuts) * self.width
        return pl.ds(pl.multiple_of(begin, self.width), self.width)

    def block_ref(self, block, unit, index, mine):
        piece = lax.div(unit, self.cuts)
        if mine:
            return self.own.at[self.part(piece), self.span(unit, index)]
        return self.held.at[block, self.part(piece), self.span(unit, index)]

    def row_ref(self, owner, target, unit):
        half = self.row_count // 2
        other = lax.rem(owner + target, 2)
        base = target + other * (1 - 2 * lax.rem(target, 2))
        slot = lax.div(lax.rem(owner - base + self.row_count, self.row_count), 2) + other * half
        begin = pl.multiple_of(slot * self.depth, self.depth)
        piece = lax.div(unit, self.cuts)
        return self.rows.at[piece, pl.ds(begin, self.depth), self.span(unit)]

    def chain_ref(self, unit, part):
        return self.rows.at[lax.div(unit, self.cuts), :, self.span(unit)]


class Chunks(Spread):
    def __init__(self, row_count, col_count, parts, own, rows, held, sems):
        super().__init__(row_count, col_count, own, rows, held, sems)
        self.chunks = rows.shape[0] // parts
        self.depth = own.shape[0] // parts
        self.width = own.shape[1] // (self.chunks * self.share)

    def plain(self, unit):
        return lax.rem(unit, self.chunks) < self.chunks * PLAIN_CHUNKS // 8

    def block_ref(self, block, unit, index, mine):
        if mine:
            lines = lax.div(unit, self.chunks) * self.depth
            begin = (index * self.chunks + lax.rem(unit, self.chunks)) * self.width
            return self.own.at[
                pl.ds(pl.multiple_of(lines, self.depth), self.depth),
                pl.ds(pl.multiple_of(begin, self.width), self.width),
            ]
        return self.held.at[block, unit, index]

    def row_ref(self, owner, target, unit):
        begin = pl.multiple_of(owner * self.depth, self.depth)
        return self.rows.at[unit, pl.ds(begin, self.depth), :]

    def chain_ref(self, unit, part):
        size = self.rows.shape[1] // self.parts
        return self.rows.at[unit, pl.ds(part * size, size), :]


def spread_sems(row_count, col_count, pieces, parts):
    share = row_count // col_count
    return [
        pltpu.SemaphoreType.DMA((2, col_count, pieces, share)),
        pltpu.SemaphoreType.DMA((2, col_count, pieces, share)),
        pltpu.SemaphoreType.DMA((col_count, share, pieces)),
        pltpu.SemaphoreType.DMA((row_count, pieces)),
        pltpu.SemaphoreType.DMA((pieces,)),
        pltpu.SemaphoreType.DMA((pieces, parts)),
        pltpu.SemaphoreType.DMA((pieces, parts)),
    ]


class Columns:
    def __init__(self, row_count, pieces, own, cols, sems):
        self.row_count, self.pieces, self.own, self.cols = row_count, pieces, own, cols
        self.load, self.send, self.recv, self.send_on = sems
        self.me_row = lax.axis_index("row")
        self.partner = self.me_row + 1 - 2 * lax.rem(self.me_row, 2)
        self.depth = own.shape[0] // pieces

    def part(self, piece):
        return pl.ds(pl.multiple_of(piece * self.depth, self.depth), self.depth)

    def copy(self, owner, target, sem, piece, src=None):
        dst = self.cols.at[owner, self.part(piece), :]
        return pltpu.make_async_remote_copy(
            src_ref=dst if src is None else src,
            dst_ref=dst,
            send_sem=sem,
            recv_sem=self.recv.at[owner, piece],
            device_id={"row": target},
            device_id_type=MESH,
        )

    def peers(self):
        peers = [(0, self.partner)]
        for step in range(1, self.row_count // 2):
            peers.append((step, lax.rem(self.me_row + 2 * step, self.row_count)))
        return peers

    def first(self, slot, target, piece, src):
        return self.copy(self.me_row, target, self.send.at[slot, piece], piece, src)

    def begin(self, piece, src):
        for slot, target in self.peers():
            self.first(slot, target, piece, src).start()

    def arrive(self, piece):
        for slot, owner in self.peers()[1:]:
            self.copy(owner, self.partner, self.send_on.at[slot, piece], piece).wait_recv()
            self.copy(owner, self.partner, self.send_on.at[slot, piece], piece).start()

    def finish(self, piece, src):
        for slot, target in self.peers():
            self.first(slot, target, piece, src).wait_send()
        self.copy(self.partner, self.partner, self.send.at[0, piece], piece).wait_recv()
        for slot, owner in self.peers()[1:]:
            self.copy(owner, self.partner, self.send_on.at[slot, piece], piece).wait_send()
            theirs = lax.rem(self.partner + 2 * slot, self.row_count)
            self.copy(theirs, self.partner, self.send.at[0, piece], piece).wait_recv()


def columns_sems(row_count, pieces):
    return [
        pltpu.SemaphoreType.DMA((pieces,)),
        pltpu.SemaphoreType.DMA((row_count // 2, pieces)),
        pltpu.SemaphoreType.DMA((row_count, pieces)),
        pltpu.SemaphoreType.DMA((row_count // 2, pieces)),
    ]


def right_loads(parts, y_cols, right, sems):
    owners, full, _ = y_cols.shape
    size = full // parts
    return [
        pltpu.make_async_copy(
            y_cols.at[owner, pl.ds(part * size, size), :],
            right.at[pl.ds((part * owners + owner) * size, size), :],
            sems.at[part * owners + owner],
        )
        for part in range(parts)
        for owner in range(owners)
    ]


def chunk_loads(parts, y_rows, index, chunk_ref, sems):
    units, size, _ = y_rows.shape
    return [
        pltpu.make_async_copy(
            y_rows.at[part * (units // parts) + index],
            chunk_ref.at[pl.ds(part * size, size), :],
            sems.at[part],
        )
        for part in range(parts)
    ]


def turn(chunk_ref, turned, gap_rows, gap_turned, begin):
    rows = turned.shape[0]
    turned[...] = chunk_ref[...].T
    gaps = gap_rows[:, pl.ds(pl.multiple_of(begin, rows), rows)]
    gap_turned[...] = jnp.broadcast_to(gaps, (128, rows)).T


def quotient(turned, right, gap_turned, gap_cols, span):
    gram = jnp.dot(turned[...], right, preferred_element_type=jnp.float32)
    copies = gram.shape[1] // 128
    total = jnp.concatenate([gap_turned[...]] * copies, axis=1) + gap_cols[:, span]
    return (-gram / total).astype(jnp.bfloat16)


def dress_kernel(
    row_count, col_count, pieces, cuts, parts, chunks, ready, amplitudes, own, gap_rows, gap_cols,
    held, held_y, y_rows, y_cols, done, dressed, table, rows, mine, kept,
    to_partner, from_partner, to_peer, from_peer, chol, chunk_buf, turned, gap_turned, staged,
    table_sem, chol_sem, partner_send, partner_recv, peer_send, peer_recv,
    right_sem, chunk_sem, staged_sem, *sems
):
    gather = Gather(row_count, col_count, pieces, cuts, own, rows, held, sems[:7])
    full = dressed.shape[0]
    flow = Chunks(row_count, col_count, parts, dressed, y_rows, held_y, sems[7:14])
    columns = Columns(row_count, pieces, dressed, y_cols, sems[14:])
    me_row, depth = gather.me_row, gather.depth
    partner = me_row + 1 - 2 * lax.rem(me_row, 2)
    half = row_count // 2
    split = table_sem.shape[0]
    chunk = table.shape[0] // split
    tile = min(512, table.shape[1])
    tiles = table.shape[1] // tile

    def table_copy(index):
        span = pl.ds(index * chunk, chunk)
        return pltpu.make_async_copy(
            amplitudes.at[span, :], table.at[span, :], table_sem.at[index]
        )

    def chol_copy(piece):
        return pltpu.make_async_copy(
            own.at[gather.part(piece), :], chol.at[piece], chol_sem.at[piece]
        )

    def partner_copy(piece):
        return pltpu.make_async_remote_copy(
            src_ref=to_partner.at[lax.rem(piece, 2)],
            dst_ref=from_partner.at[piece],
            send_sem=partner_send.at[piece],
            recv_sem=partner_recv.at[piece],
            device_id={"row": partner},
            device_id_type=MESH,
        )

    def peer_copy(step, piece):
        return pltpu.make_async_remote_copy(
            src_ref=to_peer.at[lax.rem(piece, 2), step - 1],
            dst_ref=from_peer.at[piece, half - step - 1],
            send_sem=peer_send.at[piece, step],
            recv_sem=peer_recv.at[piece, half - step],
            device_id={"row": lax.rem(me_row + 2 * step, row_count)},
            device_id_type=MESH,
        )

    def multiply(piece, cut):
        @pl.when(jnp.logical_and(cut == 0, piece >= 2))
        def _():
            partner_copy(piece - 2).wait_send()

        @pl.loop(0, tiles // cuts)
        def _(index):
            begin = (cut * (tiles // cuts) + index) * tile
            span = pl.ds(pl.multiple_of(begin, tile), tile)
            product = jnp.dot(
                rows[piece], table[:, span], preferred_element_type=jnp.float32
            )
            mine[:, span] = product[: half * depth]
            to_partner[lax.rem(piece, 2), :, span] = product[half * depth :].astype(jnp.bfloat16)

        @pl.when(cut == cuts - 1)
        def _():
            partner_copy(piece).start()

    def pair(piece):
        partner_copy(piece).wait_recv()

        @pl.when(piece >= 2)
        def _():
            for step in range(1, half):
                peer_copy(step, piece - 2).wait_send()

        @pl.loop(0, tiles)
        def _(index):
            span = pl.ds(pl.multiple_of(index * tile, tile), tile)
            both = mine[:, span] + from_partner[piece, :, span].astype(jnp.float32)
            kept[lax.rem(piece, 2), :, span] = both[:depth]
            for step in range(1, half):
                to_peer[lax.rem(piece, 2), step - 1, :, span] = both[
                    step * depth : (step + 1) * depth
                ].astype(jnp.bfloat16)

        for step in range(1, half):
            peer_copy(step, piece).start()

    def close(piece):
        chol_copy(piece).wait()
        for step in range(1, half):
            peer_copy(step, piece).wait_recv()

        @pl.loop(0, tiles)
        def _(index):
            span = pl.ds(pl.multiple_of(index * tile, tile), tile)
            total = kept[lax.rem(piece, 2), :, span]
            for step in range(1, half):
                total = total + from_peer[piece, step - 1, :, span].astype(jnp.float32)
            total = chol[piece, :, span].astype(jnp.float32) + total
            dressed[gather.part(piece), span] = total.astype(jnp.bfloat16)

    def own_y(piece):
        return dressed.at[gather.part(piece), :]

    def own_cols(piece):
        return pltpu.make_async_copy(
            own_y(piece), y_cols.at[me_row, gather.part(piece), :], columns.load.at[piece]
        )

    def right_copies():
        return right_loads(parts, y_cols, table, right_sem)

    def chunk_copies(index):
        return chunk_loads(parts, y_rows, index, chunk_buf, chunk_sem)

    def staged_copy(index, at):
        slot = lax.rem(at, 2)
        begin = pl.multiple_of(index * flow.width, flow.width)
        span = pl.ds(pl.multiple_of(at * tile, tile), tile)
        return pltpu.make_async_copy(
            staged.at[slot], done.at[pl.ds(begin, flow.width), span], staged_sem.at[slot]
        )

    def divide(index):
        for copy in chunk_copies(index):
            copy.wait()
        turn(chunk_buf, turned, gap_rows, gap_turned, index * flow.width)

        @pl.loop(0, tiles)
        def _(at):
            @pl.when(jnp.logical_or(index > 0, at >= 2))
            def _():
                staged_copy(index, at).wait()

            span = pl.ds(pl.multiple_of(at * tile, tile), tile)
            right = table[: row_count * full, span]
            staged[lax.rem(at, 2)] = quotient(turned, right, gap_turned, gap_cols, span)
            staged_copy(index, at).start()

    enter(row_count, col_count, gather.me_row, gather.me_col)
    units = pieces * cuts
    per = pieces // parts
    rate = chunks // (per * cuts)
    launch_lead = min(LAUNCH_LEAD, units)
    begin_lead = min(BEGIN_LEAD, units)
    pl.loop(0, begin_lead)(gather.begin)
    pl.loop(0, launch_lead)(gather.launch)
    for index in range(split):
        table_copy(index).start()
    for piece in range(pieces):
        chol_copy(piece).start()
    multiply_at = cuts + col_count - 2
    pair_at = multiply_at + cuts
    close_at = pair_at + CLOSE_LAG
    arrive_at = close_at + CLOSE_LAG

    def within(at, count, action):
        @pl.when(jnp.logical_and(at >= 0, at < count))
        def _():
            action(at)

    def every(at, count, action):
        @pl.when(jnp.logical_and(lax.rem(at + 8 * cuts * col_count, cuts) == 0, at >= 0))
        def _():
            within(lax.div(at, cuts), count, action)

    def finish_piece(piece):
        close(piece)
        own_cols(piece).start()
        columns.begin(piece, own_y(piece))

        @pl.when(lax.rem(piece + 1, per) == 0)
        def _():
            begin = lax.div(piece, per) * chunks
            pl.loop(begin, begin + chunks)(flow.begin)

    lag = jnp.maximum(flow.distance * jnp.where(flow.distance < 0, -1, 1), 2) + 1
    flows = parts * chunks
    flow_at = per * cuts + close_at
    last = (parts - 1) * chunks

    def advance(step):
        within(step, flows, flow.launch)
        for hops in range(1, col_count):
            within(step - hops + 1, flows, functools.partial(flow.arrive, hops))
        for distance in range(1, col_count):
            within(step - distance, flows, functools.partial(flow.relay, distance))
        at = step - lag + 1

        @pl.when(jnp.logical_and(flow.sliced(at), jnp.logical_and(at >= 0, at < flows)))
        def _():
            flow.wait_rows(at)

    @pl.loop(0, pieces * cuts + close_at)
    def _(tick):
        within(tick + begin_lead, units, gather.begin)
        within(tick + launch_lead, units, gather.launch)
        for hops in range(1, col_count):
            within(tick - hops + 1, units, functools.partial(gather.arrive, hops))
        for distance in range(1, col_count - 1):
            within(tick - distance, units, functools.partial(gather.relay, distance))
        within(tick - col_count + 1, units, gather.settle)
        every(tick - pair_at, pieces, pair)
        every(tick - close_at, pieces, finish_piece)

        @pl.when(tick == multiply_at)
        def _():
            for index in range(split):
                table_copy(index).wait()

        within(
            tick - multiply_at,
            units,
            lambda at: multiply(lax.div(at, cuts), lax.rem(at, cuts)),
        )
        every(tick - arrive_at, pieces - 1, columns.arrive)

        @pl.when(tick >= flow_at)
        def _():
            begin = (tick - flow_at) * rate
            pl.loop(begin, begin + rate)(advance)

    @pl.loop(last, flows + col_count)
    def _(step):
        at = step - lag - last
        go = jnp.logical_and(at >= 0, at < ready)

        @pl.when(go)
        def _():
            for copy in chunk_copies(at):
                copy.start()

        advance(step)

        @pl.when(step == last + 2)
        def _():
            columns.arrive(pieces - 1)
            for piece in range(pieces):
                own_cols(piece).wait()
                columns.finish(piece, own_y(piece))
            for copy in right_copies():
                copy.start()
            for copy in right_copies():
                copy.wait()

        @pl.when(go)
        def _():
            divide(at)

    for at in range(2):
        staged_copy(0, at).wait()
    for piece in range(max(pieces - 2, 0), pieces):
        partner_copy(piece).wait_send()
        for step in range(1, half):
            peer_copy(step, piece).wait_send()

    pl.loop(0, units)(gather.wait_sends)

    pl.loop(0, flows)(flow.wait_sends)


def finish_kernel(
    parts, ready, done, y_rows, y_cols, gap_rows, gap_cols, out,
    passed, right, chunk_buf, turned, gap_turned, staged,
    right_sem, chunk_sem, read_sem, write_sem, staged_sem
):
    late = chunk_buf.shape[0]
    right_copies = right_loads(parts, y_cols, right, right_sem)
    chunk_copies = [
        chunk_loads(parts, y_rows, ready + index, chunk_buf.at[index], chunk_sem.at[index])
        for index in range(late)
    ]
    rows, tile = staged.shape[1:]
    tiles = right.shape[1] // tile
    part = passed.shape[1]

    def read(index):
        begin = pl.multiple_of(index * part, part)
        return pltpu.make_async_copy(
            done.at[pl.ds(begin, part), :], passed.at[index], read_sem.at[index]
        )

    def write(index):
        begin = pl.multiple_of(index * part, part)
        return pltpu.make_async_copy(
            passed.at[index], out.at[pl.ds(begin, part), :], write_sem.at[index]
        )

    def staged_copy(index, at):
        slot = lax.rem(at, 2)
        span = pl.ds(pl.multiple_of(at * tile, tile), tile)
        return pltpu.make_async_copy(
            staged.at[slot], out.at[pl.ds((ready + index) * rows, rows), span], staged_sem.at[slot]
        )

    for copy in right_copies:
        copy.start()
    for index in range(late):
        for copy in chunk_copies[index]:
            copy.start()

    @pl.loop(0, late * tiles)
    def _(index):
        read(index).start()

    for copy in right_copies:
        copy.wait()
    for index in range(late):
        for copy in chunk_copies[index]:
            copy.wait()
        turn(chunk_buf.at[index], turned, gap_rows, gap_turned, (ready + index) * rows)

        @pl.loop(0, tiles)
        def _(at):
            read(index * tiles + at).wait()
            write(index * tiles + at).start()

            @pl.when(jnp.logical_or(index > 0, at >= 2))
            def _():
                staged_copy(index, at).wait()

            span = pl.ds(pl.multiple_of(at * tile, tile), tile)
            staged[lax.rem(at, 2)] = quotient(turned, right[:, span], gap_turned, gap_cols, span)
            staged_copy(index, at).start()

    for at in range(2):
        staged_copy(0, at).wait()

    @pl.loop(0, late * tiles)
    def _(index):
        write(index).wait()


def update(amplitudes, own, gap_rows, gap_cols, row_count, col_count, collective_id):
    depth, width = own.shape
    rows_width = amplitudes.shape[0]
    pieces = max(1, min(8, depth // 16))
    chunks = max(2, min(CHUNKS, rows_width // 128))
    tile = min(512, width)
    cuts = min(CUTS, width // tile)
    parts = min(SPLIT, pieces)
    late = max(1, chunks * LATE // 8)
    ready = chunks - late
    share = row_count // col_count
    span = rows_width // chunks
    depth_piece, half = depth // pieces, row_count // 2
    bf16, f32, dma = jnp.bfloat16, jnp.float32, pltpu.SemaphoreType.DMA
    scratch = [
        pltpu.VMEM((depth, width), bf16),
        pltpu.VMEM(amplitudes.shape, bf16),
        pltpu.VMEM((pieces, row_count * depth_piece, amplitudes.shape[0]), bf16),
        pltpu.VMEM((half * depth_piece, width), f32),
        pltpu.VMEM((2, depth_piece, width), f32),
        pltpu.VMEM((2, half * depth_piece, width), bf16),
        pltpu.VMEM((pieces, half * depth_piece, width), bf16),
        pltpu.VMEM((2, half - 1, depth_piece, width), bf16),
        pltpu.VMEM((pieces, half - 1, depth_piece, width), bf16),
        pltpu.VMEM((pieces, depth_piece, width), bf16),
        pltpu.VMEM((row_count * depth, span), bf16),
        pltpu.VMEM((span, row_count * depth), bf16),
        pltpu.VMEM((span, 128), f32),
        pltpu.VMEM((2, span, tile), bf16),
        dma((4,)),
        dma((pieces,)),
        dma((pieces,)),
        dma((pieces,)),
        dma((pieces, half)),
        dma((pieces, half)),
        dma((parts * row_count,)),
        dma((parts,)),
        dma((2,)),
    ]
    scratch += spread_sems(row_count, col_count, pieces * cuts, 1)
    scratch += spread_sems(row_count, col_count, parts * chunks, 2)
    scratch += columns_sems(row_count, pieces)
    anywhere = pl.BlockSpec(memory_space=pl.ANY)
    near = pl.BlockSpec(memory_space=pltpu.VMEM)
    _, _, y_rows, y_cols, done = pl.pallas_call(
        functools.partial(dress_kernel, row_count, col_count, pieces, cuts, parts, chunks, ready),
        out_shape=(
            jax.ShapeDtypeStruct((col_count, depth, width), bf16),
            jax.ShapeDtypeStruct((col_count, parts * chunks, share, depth // parts, span), bf16),
            jax.ShapeDtypeStruct((parts * chunks, row_count * depth // parts, span), bf16),
            jax.ShapeDtypeStruct((row_count, depth, width), bf16),
            jax.ShapeDtypeStruct((ready * span, width), bf16),
        ),
        in_specs=[anywhere, anywhere, near, near],
        out_specs=(anywhere,) * 5,
        scratch_shapes=scratch,
        compiler_params=pltpu.CompilerParams(
            collective_id=collective_id, has_side_effects=True, vmem_limit_bytes=67043328
        ),
        name="dress",
    )(amplitudes, own, gap_rows, gap_cols)
    moves = late * (width // tile)
    return pl.pallas_call(
        functools.partial(finish_kernel, parts, ready),
        out_shape=jax.ShapeDtypeStruct(amplitudes.shape, bf16),
        in_specs=[anywhere] * 3 + [near] * 2,
        out_specs=anywhere,
        scratch_shapes=[
            pltpu.VMEM((moves, ready * span // moves, width), bf16),
            pltpu.VMEM((row_count * depth, width), bf16),
            pltpu.VMEM((late, row_count * depth, span), bf16),
            pltpu.VMEM((span, row_count * depth), bf16),
            pltpu.VMEM((span, 128), f32),
            pltpu.VMEM((2, span, tile), bf16),
            dma((parts * row_count,)),
            dma((late, parts)),
            dma((moves,)),
            dma((moves,)),
            dma((2,)),
        ],
        compiler_params=pltpu.CompilerParams(vmem_limit_bytes=67043328),
        name="finish",
    )(done, y_rows, y_cols, gap_rows, gap_cols)


def local(row_count, col_count, amplitudes, cholesky, occ_index, vir_index, eps_occ, eps_vir):
    row_position = lax.axis_index("row")
    col_position = lax.axis_index("col")
    rows_block, cols_block = amplitudes.shape
    gap_rows = pair_gaps(
        occ_index, vir_index, eps_occ, eps_vir, row_position * rows_block, rows_block
    )
    gap_cols = pair_gaps(
        occ_index, vir_index, eps_occ, eps_vir, col_position * cols_block, cols_block
    )
    return update(
        amplitudes, cholesky, gap_rows[None, :], gap_cols[None, :], row_count, col_count, 0
    )


def solution(mesh):
    return jax.shard_map(
        functools.partial(local, mesh.shape["row"], mesh.shape["col"]),
        mesh=mesh,
        in_specs=(
            P(("grp", "row"), "col"),
            P("row", ("grp", "col")),
            P("grp"),
            P("grp"),
            P("grp"),
            P("grp"),
        ),
        out_specs=P(("grp", "row"), "col"),
        check_vma=False,
    )
```

time: 369 us -> 360 us (0.976)
  matrix products: 48.2 us -> 0 us
  Pallas kernels: 314 us -> 353 us
    dot_general x1 -> x0, matrix products: 48.2 us -> none  [local(): lax.dot_general(ydress_rows, ydress_cols, contract, preferred_element_typ...]
    pallas_call x1 -> x2, Pallas kernels: 314 us -> 353 us  [the longest x1 329 us: update(): pl.pallas_call(functools.partial(dress_kernel, row_count, col_count, piec...]
where the time goes in v2:
time: 360 us; the launch traced here: 359 us
  Pallas kernels  353 us (98%)
  other arithmetic  5.91 us (2%)
    pallas_call x1, Pallas kernels, update(): pl.pallas_call(functools.partial(dress_kernel, row_count, col_count, piec...  329 us
    pallas_call x1, Pallas kernels, update(): pl.pallas_call(functools.partial(finish_kernel, parts, ready), out_shape=...  24.1 us

profile of v2, /device:TPU:3, one launch (start us, length us, event | category | flops | bytes accessed | tf_op | source)
XLA Modules:
  0.0 359.4 jit_solution(9267716431644933607)
XLA Ops:
  0.0 0.8 fusion
  0.8 0.9 select_reduce_fusion.2
  1.7 3.8 %select_reduce_fusion = (f32[4096]{0:T(1024)S(1)}, f32[4096]{0:T(1024)S(1)}) fusion(s32[4096]{0:T(1024)S(1)} %get-tuple-element.19, f32[512]{0:T(512)} %param.11, s32[4096]{0:T(1024)S(1)} %get-tuple-element.20), kind=kLoop, calls=%fused_computation | loop fusion | flops 12574720 | bytes 67584 | tf_op jit(solution)/shard_map/reduce_sum | solution.py:30
  5.5 0.6 sub.28
  6.1 0.6 sub.26
  6.7 328.6 %dress.1 = (bf16[4,256,4096]{2,1,0:T(8,128)(2,1)}, bf16[4,16,1,128,512]{4,3,2,1,0:T(8,128)(2,1)}, bf16[16,512,512]{2,1,0:T(8,128)(2,1)}, bf16[4,256,4096]{2,1,0:T(8,128)(2,1)}, bf16[3072,4096]{1,0:T(8,128)(2,1)}) custom-call(bf16[4096,4096]{1,0:T(8,128)(2,1)} %amplitudes.1, bf16[256,4096]{1,0:T(8,128)(2,1)} %own.1, f32[1,4096]{1,0:T(1,128)} %bitcast.4, ...), custom_call_target="tpu_custom_call" | custom-call | tf_op jit(solution)/shard_map/dress/pallas_call | solution.py:806
  335.3 24.1 %finish.1 = bf16[4096,4096]{1,0:T(8,128)(2,1)} custom-call(bf16[3072,4096]{1,0:T(8,128)(2,1)} %get-tuple-element.8.done, bf16[16,512,512]{2,1,0:T(8,128)(2,1)} %get-tuple-element.9.y_rows, bf16[4,256,4096]{2,1,0:T(8,128)(2,1)} %get-tuple-element.10.y_cols, f32[1,4096]{1,0:T(1,128)} %bitcast.5, f32[1,4096]{1,0:T(1,128)} %bitcast.3), custom_call_target="tpu_custom_call" | custom-call | tf_op jit(solution)/shard_map/finish/pallas_call | solution.py:824

commit v3 on v2

--- a/solution.py
+++ b/solution.py
@@ -15,22 +15,22 @@
 PLAIN = 4
 PLAIN_CHUNKS = 4
 LAUNCH_LEAD = 1
+FLOW_LEAD = 2
 BEGIN_LEAD = 2
 CLOSE_LAG = 1
 
 
-def pair_gaps(occ_index, vir_index, eps_occ, eps_vir, begin_pair, pair_count):
-    occ_rows = lax.dynamic_slice_in_dim(occ_index, begin_pair, pair_count, 0)
-    vir_rows = lax.dynamic_slice_in_dim(vir_index, begin_pair, pair_count, 0)
-    occ_table = jnp.arange(eps_occ.shape[0], dtype=jnp.int32)
-    vir_table = jnp.arange(eps_vir.shape[0], dtype=jnp.int32)
-    occ_energy = jnp.sum(
-        jnp.where(occ_rows[:, None] == occ_table[None, :], eps_occ[None, :], 0.0), axis=1
-    )
-    vir_energy = jnp.sum(
-        jnp.where(vir_rows[:, None] == vir_table[None, :], eps_vir[None, :], 0.0), axis=1
-    )
-    return vir_energy - occ_energy
+def picked(index_ref, table):
+    wanted = index_ref[...]
+    width = 8 if table.shape[0] % 8 == 0 else 1
+
+    def pick(step, total):
+        for offset in range(width):
+            at = step * width + offset
+            total = jnp.where(wanted == at, table[at], total)
+        return total
+
+    return lax.fori_loop(0, table.shape[0] // width, pick, jnp.zeros(wanted.shape, jnp.float32))
 
 
 def enter(row_count, col_count, me_row, me_col):
@@ -409,25 +409,27 @@
     ]
 
 
-def turn(chunk_ref, turned, gap_rows, gap_turned, begin):
-    rows = turned.shape[0]
+def turn(chunk_ref, turned, gap_rows, gap_turned, index):
     turned[...] = chunk_ref[...].T
-    gaps = gap_rows[:, pl.ds(pl.multiple_of(begin, rows), rows)]
-    gap_turned[...] = jnp.broadcast_to(gaps, (128, rows)).T
-
-
-def quotient(turned, right, gap_turned, gap_cols, span):
+    lines = turned.shape[0] // 128
+    for line in range(lines):
+        gaps = gap_rows[pl.ds(index * lines + line, 1), :]
+        gap_turned[pl.ds(line * 128, 128), :] = jnp.broadcast_to(gaps, (128, 128)).T
+
+
+def quotient(turned, right, gap_turned, gap_cols, at):
     gram = jnp.dot(turned[...], right, preferred_element_type=jnp.float32)
-    copies = gram.shape[1] // 128
-    total = jnp.concatenate([gap_turned[...]] * copies, axis=1) + gap_cols[:, span]
+    lines = gram.shape[1] // 128
+    gaps = [gap_cols[pl.ds(at * lines + line, 1), :] for line in range(lines)]
+    total = jnp.concatenate([gap_turned[...] + line for line in gaps], axis=1)
     return (-gram / total).astype(jnp.bfloat16)
 
 
 def dress_kernel(
-    row_count, col_count, pieces, cuts, parts, chunks, ready, amplitudes, own, gap_rows, gap_cols,
-    held, held_y, y_rows, y_cols, done, dressed, table, rows, mine, kept,
+    row_count, col_count, pieces, cuts, parts, chunks, ready, amplitudes, own, occ_index, vir_index, eps_occ, eps_vir,
+    held, held_y, y_rows, y_cols, done, gap_rows, gap_cols, dressed, table, rows, mine, kept,
     to_partner, from_partner, to_peer, from_peer, chol, chunk_buf, turned, gap_turned, staged,
-    table_sem, chol_sem, partner_send, partner_recv, peer_send, peer_recv,
+    row_indices, col_indices, index_sem, table_sem, chol_sem, partner_send, partner_recv, peer_send, peer_recv,
     right_sem, chunk_sem, staged_sem, *sems
 ):
     gather = Gather(row_count, col_count, pieces, cuts, own, rows, held, sems[:7])
@@ -552,7 +554,7 @@
     def divide(index):
         for copy in chunk_copies(index):
             copy.wait()
-        turn(chunk_buf, turned, gap_rows, gap_turned, index * flow.width)
+        turn(chunk_buf, turned, gap_rows, gap_turned, index)
 
         @pl.loop(0, tiles)
         def _(at):
@@ -562,21 +564,41 @@
 
             span = pl.ds(pl.multiple_of(at * tile, tile), tile)
             right = table[: row_count * full, span]
-            staged[lax.rem(at, 2)] = quotient(turned, right, gap_turned, gap_cols, span)
+            staged[lax.rem(at, 2)] = quotient(turned, right, gap_turned, gap_cols, at)
             staged_copy(index, at).start()
 
     enter(row_count, col_count, gather.me_row, gather.me_col)
     units = pieces * cuts
     per = pieces // parts
     rate = chunks // (per * cuts)
+    flow_lead = min(FLOW_LEAD, rate)
     launch_lead = min(LAUNCH_LEAD, units)
     begin_lead = min(BEGIN_LEAD, units)
     pl.loop(0, begin_lead)(gather.begin)
+    pairs = ((row_indices, gather.me_row, gap_rows), (col_indices, gather.me_col, gap_cols))
+
+    def index_copies(side):
+        indices, block, _ = pairs[side]
+        lines = indices.shape[1]
+        span = pl.ds(pl.multiple_of(block * lines, lines), lines)
+        return [
+            pltpu.make_async_copy(source.at[span, :], indices.at[kind], index_sem.at[side, kind])
+            for kind, source in enumerate((occ_index, vir_index))
+        ]
+
+    for side in range(2):
+        for copy in index_copies(side):
+            copy.start()
     pl.loop(0, launch_lead)(gather.launch)
     for index in range(split):
         table_copy(index).start()
     for piece in range(pieces):
         chol_copy(piece).start()
+    for side in range(2):
+        indices, _, gaps = pairs[side]
+        for copy in index_copies(side):
+            copy.wait()
+        gaps[...] = picked(indices.at[1], eps_vir) - picked(indices.at[0], eps_occ)
     multiply_at = cuts + col_count - 2
     pair_at = multiply_at + cuts
     close_at = pair_at + CLOSE_LAG
@@ -597,10 +619,9 @@
         own_cols(piece).start()
         columns.begin(piece, own_y(piece))
 
-        @pl.when(lax.rem(piece + 1, per) == 0)
-        def _():
-            begin = lax.div(piece, per) * chunks
-            pl.loop(begin, begin + chunks)(flow.begin)
+        @pl.when(piece == per - 1)
+        def _():
+            pl.loop(0, flow_lead)(flow.begin)
 
     lag = jnp.maximum(flow.distance * jnp.where(flow.distance < 0, -1, 1), 2) + 1
     flows = parts * chunks
@@ -608,11 +629,12 @@
     last = (parts - 1) * chunks
 
     def advance(step):
-        within(step, flows, flow.launch)
         for hops in range(1, col_count):
             within(step - hops + 1, flows, functools.partial(flow.arrive, hops))
         for distance in range(1, col_count):
             within(step - distance, flows, functools.partial(flow.relay, distance))
+        within(step + flow_lead, flows, flow.begin)
+        within(step, flows, flow.launch)
         at = step - lag + 1
 
         @pl.when(jnp.logical_and(flow.sliced(at), jnp.logical_and(at >= 0, at < flows)))
@@ -621,12 +643,12 @@
 
     @pl.loop(0, pieces * cuts + close_at)
     def _(tick):
-        within(tick + begin_lead, units, gather.begin)
-        within(tick + launch_lead, units, gather.launch)
         for hops in range(1, col_count):
             within(tick - hops + 1, units, functools.partial(gather.arrive, hops))
         for distance in range(1, col_count - 1):
             within(tick - distance, units, functools.partial(gather.relay, distance))
+        within(tick + begin_lead, units, gather.begin)
+        within(tick + launch_lead, units, gather.launch)
         within(tick - col_count + 1, units, gather.settle)
         every(tick - pair_at, pieces, pair)
         every(tick - close_at, pieces, finish_piece)
@@ -736,7 +758,7 @@
     for index in range(late):
         for copy in chunk_copies[index]:
             copy.wait()
-        turn(chunk_buf.at[index], turned, gap_rows, gap_turned, (ready + index) * rows)
+        turn(chunk_buf.at[index], turned, gap_rows, gap_turned, ready + index)
 
         @pl.loop(0, tiles)
         def _(at):
@@ -748,7 +770,7 @@
                 staged_copy(index, at).wait()
 
             span = pl.ds(pl.multiple_of(at * tile, tile), tile)
-            staged[lax.rem(at, 2)] = quotient(turned, right[:, span], gap_turned, gap_cols, span)
+            staged[lax.rem(at, 2)] = quotient(turned, right[:, span], gap_turned, gap_cols, at)
             staged_copy(index, at).start()
 
     for at in range(2):
@@ -759,7 +781,9 @@
         write(index).wait()
 
 
-def update(amplitudes, own, gap_rows, gap_cols, row_count, col_count, collective_id):
+def update(
+    amplitudes, own, occ_index, vir_index, eps_occ, eps_vir, row_count, col_count, collective_id
+):
     depth, width = own.shape
     rows_width = amplitudes.shape[0]
     pieces = max(1, min(8, depth // 16))
@@ -788,6 +812,9 @@
         pltpu.VMEM((span, row_count * depth), bf16),
         pltpu.VMEM((span, 128), f32),
         pltpu.VMEM((2, span, tile), bf16),
+        pltpu.VMEM((2, rows_width // 128, 128), jnp.int32),
+        pltpu.VMEM((2, width // 128, 128), jnp.int32),
+        dma((2, 2)),
         dma((4,)),
         dma((pieces,)),
         dma((pieces,)),
@@ -803,7 +830,8 @@
     scratch += columns_sems(row_count, pieces)
     anywhere = pl.BlockSpec(memory_space=pl.ANY)
     near = pl.BlockSpec(memory_space=pltpu.VMEM)
-    _, _, y_rows, y_cols, done = pl.pallas_call(
+    table = pl.BlockSpec(memory_space=pltpu.SMEM)
+    _, _, y_rows, y_cols, done, gap_rows, gap_cols = pl.pallas_call(
         functools.partial(dress_kernel, row_count, col_count, pieces, cuts, parts, chunks, ready),
         out_shape=(
             jax.ShapeDtypeStruct((col_count, depth, width), bf16),
@@ -811,15 +839,17 @@
             jax.ShapeDtypeStruct((parts * chunks, row_count * depth // parts, span), bf16),
             jax.ShapeDtypeStruct((row_count, depth, width), bf16),
             jax.ShapeDtypeStruct((ready * span, width), bf16),
+            jax.ShapeDtypeStruct((rows_width // 128, 128), f32),
+            jax.ShapeDtypeStruct((width // 128, 128), f32),
         ),
-        in_specs=[anywhere, anywhere, near, near],
-        out_specs=(anywhere,) * 5,
+        in_specs=[anywhere] * 4 + [table] * 2,
+        out_specs=(anywhere,) * 5 + (near,) * 2,
         scratch_shapes=scratch,
         compiler_params=pltpu.CompilerParams(
             collective_id=collective_id, has_side_effects=True, vmem_limit_bytes=67043328
         ),
         name="dress",
-    )(amplitudes, own, gap_rows, gap_cols)
+    )(amplitudes, own, occ_index, vir_index, eps_occ, eps_vir)
     moves = late * (width // tile)
     return pl.pallas_call(
         functools.partial(finish_kernel, parts, ready),
@@ -845,17 +875,9 @@
 
 
 def local(row_count, col_count, amplitudes, cholesky, occ_index, vir_index, eps_occ, eps_vir):
-    row_position = lax.axis_index("row")
-    col_position = lax.axis_index("col")
-    rows_block, cols_block = amplitudes.shape
-    gap_rows = pair_gaps(
-        occ_index, vir_index, eps_occ, eps_vir, row_position * rows_block, rows_block
-    )
-    gap_cols = pair_gaps(
-        occ_index, vir_index, eps_occ, eps_vir, col_position * cols_block, cols_block
-    )
     return update(
-        amplitudes, cholesky, gap_rows[None, :], gap_cols[None, :], row_count, col_count, 0
+        amplitudes, cholesky, occ_index.reshape(-1, 128), vir_index.reshape(-1, 128),
+        eps_occ, eps_vir, row_count, col_count, 0,
     )
 
 

time: 360 us -> 339 us (0.942)
  Pallas kernels: 353 us -> 338 us
  other arithmetic: 5.91 us -> 0 us
    pallas_call x1, Pallas kernels: 329 us -> 314 us  [update(): pl.pallas_call(functools.partial(dress_kernel, row_count, col_count, piec...]
    reduce_sum x2 -> x0, other arithmetic: 4.71 us -> none  [the longest x1 3.81 us: pair_gaps(): jnp.sum(jnp.where(vir_rows[:, None] == vir_table[None, :], eps_vir[None,...]
where the time goes in v3:
time: 339 us; the launch traced here: 338 us
  Pallas kernels  338 us (100%)
    pallas_call x1, Pallas kernels, update(): pl.pallas_call(functools.partial(dress_kernel, row_count, col_count, piec...  314 us
    pallas_call x1, Pallas kernels, update(): pl.pallas_call(functools.partial(finish_kernel, parts, ready), out_shape=...  24.3 us

profile of v3, /device:TPU:3, one launch (start us, length us, event | category | flops | bytes accessed | tf_op | source)
XLA Modules:
  0.0 338.2 jit_solution(12848509820568302759)
XLA Ops:
  0.0 313.9 %dress.1 = (bf16[4,256,4096]{2,1,0:T(8,128)(2,1)}, bf16[4,16,1,128,512]{4,3,2,1,0:T(8,128)(2,1)}, bf16[16,512,512]{2,1,0:T(8,128)(2,1)}, bf16[4,256,4096]{2,1,0:...) custom-call(bf16[4096,4096]{1,0:T(8,128)(2,1)} %amplitudes.1, ...), custom_call_target="tpu_custom_call" | custom-call | tf_op jit(solution)/shard_map/dress/pallas_call | solution.py:834
  313.9 24.3 %finish.1 = bf16[4096,4096]{1,0:T(8,128)(2,1)} custom-call(bf16[3072,4096]{1,0:T(8,128)(2,1)} %get-tuple-element.10.done, bf16[16,512,512]{2,1,0:T(8,128)(2,1)} %get-tuple-element.11.y_rows, bf16[4,256,4096]{2,1,0:T(8,128)(2,1)} %get-tuple-element.12.y_cols, f32[32,128]{1,0:T(8,128)} %get-tuple-element.13.gap_rows, f32[32,128]{1,0:T(8,128)} %get-tuple-element.14.gap_cols), custom_call_target="tpu_custom_call" | custom-call | tf_op jit(solution)/shard_map/finish/pallas_call | solution.py:854

commit v4 on v3

--- a/solution.py
+++ b/solution.py
@@ -16,7 +16,7 @@
 PLAIN_CHUNKS = 4
 LAUNCH_LEAD = 1
 FLOW_LEAD = 2
-BEGIN_LEAD = 2
+BEGIN_LEAD = 3
 CLOSE_LAG = 1
 
 

time: 339 us -> 338 us (level)
  no operation moved by 1% of the time
where the time goes in v4:
time: 338 us
  Pallas kernels  338 us (100%)
    pallas_call x1, Pallas kernels, update(): pl.pallas_call(functools.partial(dress_kernel, row_count, col_count, piec...  314 us
    pallas_call x1, Pallas kernels, update(): pl.pallas_call(functools.partial(finish_kernel, parts, ready), out_shape=...  24.1 us

profile of v4, /device:TPU:3, one launch (start us, length us, event | category | flops | bytes accessed | tf_op | source)
XLA Modules:
  0.0 337.9 jit_solution(5186754839584070614)
XLA Ops:
  0.0 313.8 %dress.1 = (bf16[4,256,4096]{2,1,0:T(8,128)(2,1)}, bf16[4,16,1,128,512]{4,3,2,1,0:T(8,128)(2,1)}, bf16[16,512,512]{2,1,0:T(8,128)(2,1)}, bf16[4,256,4096]{2,1,0:...) custom-call(bf16[4096,4096]{1,0:T(8,128)(2,1)} %amplitudes.1, ...), custom_call_target="tpu_custom_call" | custom-call | tf_op jit(solution)/shard_map/dress/pallas_call | solution.py:834
  313.8 24.1 %finish.1 = bf16[4096,4096]{1,0:T(8,128)(2,1)} custom-call(bf16[3072,4096]{1,0:T(8,128)(2,1)} %get-tuple-element.10.done, bf16[16,512,512]{2,1,0:T(8,128)(2,1)} %get-tuple-element.11.y_rows, bf16[4,256,4096]{2,1,0:T(8,128)(2,1)} %get-tuple-element.12.y_cols, f32[32,128]{1,0:T(8,128)} %get-tuple-element.13.gap_rows, f32[32,128]{1,0:T(8,128)} %get-tuple-element.14.gap_cols), custom_call_target="tpu_custom_call" | custom-call | tf_op jit(solution)/shard_map/finish/pallas_call | solution.py:854
